TPU v7x, 512 devices: a whole 4x4x16 slice. The times are simulated.
512 devices in a mesh: tm: 8 (over x, core), dp: 64 (over z, y).
Axes of the slice: x: 4, y: 4, z: 16, core: 2. Of those that a mesh axis runs over, the one named last changes fastest.
Arguments:
- edge_feat: bfloat16 [8, 8192, 186], P('tm', 'dp'), may hold values from -6 to 6
- endpoint_slots: int32 [8, 2, 8192], P('tm', None, 'dp'), may hold values from 0 to 2047, as said below
- neighbor_slots: int32 [8, 20, 8192], P('tm', None, 'dp'), may hold values from 0 to 2047, as said below
- neighbor_gap: int32 [8, 20, 8192], P('tm', None, 'dp'), may hold values from 0 to 999
- score_grad: float32 [8, 8192], P('tm', 'dp'), may hold values from -1.5 to 1.5
- node_list: int32 [8, 64, 2048], P('tm', 'dp'), may hold values from 0 to 128, as said below
- memory0: float32 [8192, 256], P('dp'), may hold values from -6 to 6
- msg_weight: bfloat16 [186, 256], replicated, may hold values from -0.4375 to 0.4375
- gate_weight: bfloat16 [256, 512], replicated, may hold values from -0.375 to 0.375
- gate_bias: float32 [512], replicated, may hold values from -4 to 4
- omega: float32 [256], replicated, may hold values from 0.001 to 1
- attn_weights: bfloat16 [4, 256, 256], replicated, may hold values from -0.375 to 0.375
- pred_weights: bfloat16 [2, 256, 256], replicated, may hold values from -0.375 to 0.375
- pred_out: float32 [256], replicated, may hold values from -0.375 to 0.375
Outputs:
- scores: float32 [8, 8192], P('tm', 'dp')
- new_memory: float32 [8, 8192, 256], P('tm', 'dp')
- grad_out_proj: float32 [256, 256], replicated
- grad_pred: float32 [2, 256, 256], replicated
Inputs may be any that keep to these rules, and one draw needn't show every extreme that they name: `node_list`: each block of 32 slots (one device's requests to one owner) holds distinct rows first and 128 in the empty slots after them; every block holds at least one row; in each mini-batch some owner's block is full from every device. `endpoint_slots`: every slot points at a non-empty entry of its device's node list. `neighbor_slots`: every slot points at a non-empty entry of its device's node list.
All inputs are finite; a program needn't handle non-finite values.
Results may differ from a plain program's by a relative error of at most 0.017.
Values may be sent and summed in bfloat16 or wider, within the bound.
No kernel may reach another device: no remote copies, remote signals or barrier semaphores. Data moves between devices by JAX's collectives and lax.ppermute only.
A program may use at most 64 MiB of HBM per device.

v0:
```python
import math
import jax
import jax.numpy as jnp
from jax import lax
from jax.sharding import PartitionSpec as P

HEADS = 2


def shifted(value, axis, steps):
    count = lax.axis_size(axis)
    initial, last = (max(0, -steps), min(count, count - steps))
    return lax.ppermute(value, axis, [(source, source + steps) for source in range(initial, last)])


def local_step(
    slot_rows,
    end_slots,
    near_slots,
    near_gaps,
    cot_rows,
    omega,
    attn_weights,
    pred_weights,
    pred_out,
):
    feat_width = slot_rows.shape[1]
    events = end_slots.shape[1]
    near_count = near_slots.shape[0] // 2
    head_dim = feat_width // HEADS
    self_rows = jnp.take(slot_rows, end_slots, axis=0)
    near_rows = jnp.take(slot_rows, near_slots, axis=0).reshape(2, near_count, events, feat_width)
    phases = near_gaps.reshape(2, near_count, events).astype(jnp.float32)[..., None] * omega
    near_feat = (near_rows.astype(jnp.float32) + jnp.cos(phases)).astype(jnp.bfloat16)
    query_proj = jnp.einsum(
        "pea,ab->peb", self_rows, attn_weights[0], preferred_element_type=jnp.float32
    )
    key_proj = jnp.einsum(
        "pkea,ab->pkeb", near_feat, attn_weights[1], preferred_element_type=jnp.float32
    )
    value_proj = jnp.einsum(
        "pkea,ab->pkeb", near_feat, attn_weights[2], preferred_element_type=jnp.float32
    )
    query_heads = query_proj.reshape(2, 1, events, HEADS, head_dim)
    key_heads = key_proj.reshape(2, near_count, events, HEADS, head_dim)
    value_heads = value_proj.reshape(2, near_count, events, HEADS, head_dim)
    att_logits = jnp.sum(query_heads * key_heads, axis=-1) / math.sqrt(head_dim)
    weights_att = jax.nn.softmax(att_logits, axis=1)
    mixed_heads = (
        jnp.sum(weights_att[..., None] * value_heads, axis=1)
        .reshape(2, events, feat_width)
        .astype(jnp.bfloat16)
    )
    state_full = self_rows.astype(jnp.float32) + jnp.einsum(
        "pea,ab->peb", mixed_heads, attn_weights[3], preferred_element_type=jnp.float32
    )
    state_bf = state_full.astype(jnp.bfloat16)
    pre_pred = jnp.dot(state_bf[0], pred_weights[0], preferred_element_type=jnp.float32) + jnp.dot(
        state_bf[1], pred_weights[1], preferred_element_type=jnp.float32
    )
    sigmoid_pre = jax.nn.sigmoid(pre_pred)
    logit_out = jnp.sum(pre_pred * sigmoid_pre * pred_out, axis=-1)
    grad_pre = (
        cot_rows[:, None] * pred_out * (sigmoid_pre * (1.0 + pre_pred * (1.0 - sigmoid_pre)))
    ).astype(jnp.bfloat16)
    grad_first = jnp.einsum("ea,eb->ab", state_bf[0], grad_pre, preferred_element_type=jnp.float32)
    grad_second = jnp.einsum("ea,eb->ab", state_bf[1], grad_pre, preferred_element_type=jnp.float32)
    grad_state = jnp.einsum(
        "eb,pab->pea", grad_pre, pred_weights, preferred_element_type=jnp.float32
    ).astype(jnp.bfloat16)
    grad_out_proj = jnp.einsum(
        "pea,peb->ab", mixed_heads, grad_state, preferred_element_type=jnp.float32
    )
    return (logit_out, grad_out_proj, jnp.stack([grad_first, grad_second]))


def per_device(
    edge_feat,
    endpoint_slots,
    neighbor_slots,
    neighbor_gap,
    score_grad,
    node_list,
    memory0,
    msg_weight,
    gate_weight,
    gate_bias,
    omega,
    attn_weights,
    pred_weights,
    pred_out,
):
    groups = lax.axis_size("dp")
    node_dev, feat_width = memory0.shape
    list_len = node_list.shape[2]
    per_owner = list_len // groups
    requests = node_list[0, 0].reshape(groups, per_owner)
    wanted = lax.all_to_all(requests, "dp", split_axis=0, concat_axis=0, tiled=True)
    message = jnp.dot(edge_feat[0], msg_weight, preferred_element_type=jnp.float32).astype(
        jnp.bfloat16
    )
    message_wide = message.astype(jnp.float32)
    end_slots = endpoint_slots[0]
    flat_ends = end_slots.reshape(-1)
    slot_sums = (
        jnp.zeros((list_len, feat_width), jnp.float32)
        .at[flat_ends]
        .add(jnp.concatenate([message_wide, message_wide]))
    )
    slot_tally = jnp.zeros((list_len,), jnp.float32).at[flat_ends].add(1.0)
    got_sums, got_tally = (
        lax.all_to_all(
            slot_sums.reshape(groups, per_owner, feat_width),
            "dp",
            split_axis=0,
            concat_axis=0,
            tiled=True,
        ),
        lax.all_to_all(
            slot_tally.reshape(groups, per_owner), "dp", split_axis=0, concat_axis=0, tiled=True
        ),
    )
    picker = (wanted.reshape(-1)[:, None] == jnp.arange(node_dev)[None, :]).astype(jnp.bfloat16)
    flat_sums = got_sums.reshape(-1, feat_width)
    sums_high = flat_sums.astype(jnp.bfloat16)
    sums_low = (flat_sums - sums_high.astype(jnp.float32)).astype(jnp.bfloat16)
    totals = jnp.einsum(
        "sn,sd->nd", picker, sums_high, preferred_element_type=jnp.float32
    ) + jnp.einsum("sn,sd->nd", picker, sums_low, preferred_element_type=jnp.float32)
    counts = jnp.dot(
        got_tally.reshape(-1), picker.astype(jnp.float32), precision=lax.Precision.HIGHEST
    )
    touched = (counts > 0.5).astype(jnp.float32)
    mean_msg = (totals / jnp.maximum(counts, 1.0)[:, None]).astype(jnp.bfloat16)
    pre_gate = jnp.dot(mean_msg, gate_weight, preferred_element_type=jnp.float32) + gate_bias
    update = jax.nn.sigmoid(pre_gate[:, :feat_width]) * touched[:, None]
    candidate = jnp.tanh(pre_gate[:, feat_width:])
    decay_rate = 1.0 - update
    inject = update * candidate
    section_index = lax.axis_index("tm")
    before = memory0
    for relay_step in range(lax.axis_size("tm") - 1):
        moved_state = shifted((decay_rate * before + inject).astype(jnp.bfloat16), "tm", 1).astype(
            jnp.float32
        )
        before = jnp.where(section_index == 0, memory0, moved_state)
    new_memory = decay_rate * before + inject
    memory_bf = before.astype(jnp.bfloat16)
    full_table = lax.all_gather(memory_bf, "dp", axis=0, tiled=True)
    owner_of = jnp.arange(list_len, dtype=jnp.int32) // per_owner
    global_row = owner_of * node_dev + jnp.minimum(node_list[0, 0], node_dev - 1)
    slot_rows = jnp.take(full_table, global_row, axis=0)
    logit_out, grad_out, grad_pair = local_step(
        slot_rows,
        end_slots,
        neighbor_slots[0],
        neighbor_gap[0],
        score_grad[0],
        omega,
        attn_weights,
        pred_weights,
        pred_out,
    )
    grad_out, grad_pair = lax.psum((grad_out, grad_pair), ("tm", "dp"))
    return (logit_out[None, :], new_memory[None], grad_out, grad_pair)


def solution(mesh):
    in_specs = (
        P("tm", "dp", None),
        P("tm", None, "dp"),
        P("tm", None, "dp"),
        P("tm", None, "dp"),
        P("tm", "dp"),
        P("tm", "dp", None),
        P("dp", None),
        P(),
        P(),
        P(),
        P(),
        P(),
        P(),
        P(),
    )
    out_specs = (P("tm", "dp"), P("tm", "dp", None), P(), P())
    return jax.shard_map(
        per_device, mesh=mesh, in_specs=in_specs, out_specs=out_specs, check_vma=False
    )
```

profile of v0, /device:TPU:2, one launch (start us, length us, event | category | flops | bytes accessed | tf_op | source)
XLA Modules:
  0.0 856.8 jit_solution(11601709572848172272)
XLA Ops:
  7.7 1.4 broadcast_minimum_fusion
  9.1 0.7 all_to_all.15
  9.8 18.7 %all-to-all-start = ((s32[64,1,32]{2,1,0:T(1,128)}), s32[64,1,32]{2,1,0:T(1,128)S(1)}, u32[]{:S(2)}, u32[]{:S(2)}) async-start(s32[64,1,32]{2,1,0:T(1,128)} %bitcast.2), calls=%async_computation | async-start | bytes 65536 | tf_op jit(solution)/shard_map/all_to_all | solution.py:98
  28.5 0.7 compare_select_fusion.4
  29.2 2.0 scatter_custom_fusion.1
  31.2 0.7 all_to_all.18
  31.8 11.2 %all-to-all-done = s32[64,1,32]{2,1,0:T(1,128)S(1)} async-done(((s32[64,1,32]{2,1,0:T(1,128)}), s32[64,1,32]{2,1,0:T(1,128)S(1)}, u32[]{:S(2)}, u32[]{:S(2)}) %all-to-all-start) | async-done | bytes 8224 | tf_op jit(solution)/shard_map/all_to_all | solution.py:98
  43.0 4.6 all-to-all-start.2
  47.6 1.1 convolution_convert_fusion.1
  48.7 3.4 scatter_custom_fusion
  52.1 10.2 %all-to-all-done.2 = f32[64,1,32]{2,1,0:T(1,128)S(1)} async-done(((f32[64,1,32]{2,1,0:T(1,128)}), f32[64,1,32]{2,1,0:T(1,128)S(1)}, u32[]{:S(2)}, u32[]{:S(2)}) %all-to-all-start.2) | async-done | bytes 8224 | tf_op jit(solution)/shard_map/all_to_all | solution.py:119
  62.3 4.9 all-to-all-start.1
  67.3 0.7 reduce.12
  68.6 0.7 reduce.13
  70.0 95.7 %all-to-all-done.1 = f32[64,32,256]{2,1,0:T(8,128)S(1)} async-done(((f32[64,32,256]{2,1,0:T(8,128)}), f32[64,32,256]{2,1,0:T(8,128)S(1)}, u32[]{:S(2)}, u32[]{:S(2)}) %all-to-all-start.1) | async-done | bytes 2097184 | tf_op jit(solution)/shard_map/all_to_all | solution.py:112
  166.0 0.8 fusion.7
  166.8 1.0 convolution_add_fusion.1
  168.0 2.1 collective-permute-start
  170.0 3.6 collective-permute-done
  173.8 1.9 collective-permute-start.1
  175.7 3.7 collective-permute-done.1
  179.5 2.1 collective-permute-start.2
  181.5 3.7 collective-permute-done.2
  185.3 1.9 collective-permute-start.3
  187.2 3.7 collective-permute-done.3
  191.0 1.9 collective-permute-start.4
  192.9 3.7 collective-permute-done.4
  196.7 1.9 collective-permute-start.5
  198.6 3.7 collective-permute-done.5
  202.3 1.9 collective-permute-start.6
  204.3 3.7 collective-permute-done.6
  207.9 0.6 fusion.30
  209.0 0.8 copy.39
  209.8 0.8 copy.40
  210.7 136.2 %all-gather.2.cloned.1.call-done = bf16[8192,256]{1,0:T(8,128)(2,1)} async-done(((bf16[128,256]{1,0:T(8,128)(2,1)}), bf16[8192,256]{1,0:T(8,128)(2,1)}) %all-gather.2.cloned.1.call-update) | async-done | bytes 4194320 | tf_op jit(solution)/shard_map/all_gather | solution.py:149
  346.9 9.4 %gather_fusion = bf16[2048,256]{1,0:T(8,128)(2,1)S(1)} fusion(bf16[8192,256]{1,0:T(8,128)(2,1)} %all-gather.2.cloned.1.call-done, s32[2048]{0:T(1024)S(1)} %broadcast_clamp_fusion), kind=kCustom, calls=%fused_computation | custom fusion | bytes 2105344 | tf_op jit(solution)/shard_map/jit(_take)/gather | solution.py:152
  356.7 7.6 gather_fusion.2
  364.3 1.2 gather_fusion.1
  365.8 10.1 %add_convert_fusion = bf16[20,128,256]{2,1,0:T(8,128)(2,1)S(1)} fusion(f32[256]{0:T(256)S(1)} %copy-done.10, f32[20,128]{1,0:T(8,128)S(1)} %bitcast.137, bf16[20,128,256]{2,1,0:T(8,128)(2,1)S(1)} %bitcast.127, pred[20,128]{1,0:T(8,128)(4,1)S(1)} %compare_and_fusion), kind=kLoop, calls=%fused_computation.7 | loop fusion | flops 3276800 | bytes 2635264 | tf_op jit(solution)/shard_map/convert_element_type | solution.py:34
  376.8 1.1 multiply_reduce_fusion
  378.1 1.1 fusion.1
  379.4 0.8 multiply_reduce_fusion.2
  380.7 1.1 convolution_bitcast_fusion.2
  381.8 0.8 pad_maximum_fusion
  382.6 0.7 add_bitcast_fusion
  383.4 463.0 %all-reduce.3.cloned.1.call-done = (f32[256,256]{1,0:T(8,128)}, f32[2,256,256]{2,1,0:T(8,128)}) async-done(((f32[256,256]{1,0:T(8,128)}, f32[2,256,256]{2,1,0:T(8,128)}), (f32[256,256]{1,0:T(8,128)}, f32[2,256,256]{2,1,0:T(8,128)})) %all-reduce.3.cloned.1.call-update) | async-done | bytes 786448 | tf_op jit(solution)/shard_map/psum | solution.py:164
  846.4 1.7 copy.58
  848.1 1.9 copy.59
  (70 shorter events, 5.6 us)
Async XLA Ops:
  7.2 159.7 %copy-start = (bf16[256,512]{1,0:T(8,128)(2,1)S(1)}, bf16[256,512]{1,0:T(8,128)(2,1)}, u32[]{:S(2)}) copy-start(bf16[256,512]{1,0:T(8,128)(2,1)} %param.22) | copy-start | bytes 786436
  9.8 33.3 %all-to-all-start = ((s32[64,1,32]{2,1,0:T(1,128)}), s32[64,1,32]{2,1,0:T(1,128)S(1)}, u32[]{:S(2)}, u32[]{:S(2)}) async-start(s32[64,1,32]{2,1,0:T(1,128)} %bitcast.2), calls=%async_computation | async-start | bytes 65536 | tf_op jit(solution)/shard_map/all_to_all | solution.py:98
  43.0 19.3 %all-to-all-start.2 = ((f32[64,1,32]{2,1,0:T(1,128)}), f32[64,1,32]{2,1,0:T(1,128)S(1)}, u32[]{:S(2)}, u32[]{:S(2)}) async-start(f32[64,1,32]{2,1,0:T(1,128)} %bitcast.8), calls=%async_computation.2 | async-start | bytes 65536 | tf_op jit(solution)/shard_map/all_to_all | solution.py:119
  62.3 103.4 %all-to-all-start.1 = ((f32[64,32,256]{2,1,0:T(8,128)}), f32[64,32,256]{2,1,0:T(8,128)S(1)}, u32[]{:S(2)}, u32[]{:S(2)}) async-start(f32[64,32,256]{2,1,0:T(8,128)} %bitcast.6), calls=%async_computation.1 | async-start | bytes 4194304 | tf_op jit(solution)/shard_map/all_to_all | solution.py:112
  67.2 279.7 %all-gather.2.cloned.1.call-start = ((), (), s32[]{:S(2)}) async-start(), calls=%async_computation.3 | async-start | bytes 4259840 | tf_op jit(solution)/shard_map/all_gather | solution.py:149
  70.0 96.8 %copy-start.11 = (f32[512]{0:T(512)S(1)}, f32[512]{0:T(512)}, u32[]{:S(2)}) copy-start(f32[512]{0:T(512)} %param.23) | copy-start | bytes 6148
  166.0 1.8 copy-start.1
  167.8 41.0 %copy-start.8 = (s32[1,20,128]{2,0,1:T(1,128)S(1)}, s32[1,20,128]{2,0,1:T(1,128)}, u32[]{:S(2)}) copy-start(s32[1,20,128]{2,0,1:T(1,128)} %param.17) | copy-start | bytes 30724
  167.8 41.0 %copy-start.2 = (bf16[4,256,256]{2,1,0:T(8,128)(2,1)S(1)}, bf16[4,256,256]{2,1,0:T(8,128)(2,1)}, u32[]{:S(2)}) copy-start(bf16[4,256,256]{2,1,0:T(8,128)(2,1)} %param.25) | copy-start | bytes 1572868
  168.0 5.7 collective-permute-start
  173.8 5.6 collective-permute-start.1
  179.4 31.1 %copy-start.9 = (s32[1,2,128]{2,1,0:T(2,128)S(1)}, s32[1,2,128]{2,1,0:T(2,128)}, u32[]{:S(2)}) copy-start(s32[1,2,128]{2,1,0:T(2,128)} %param.15) | copy-start | bytes 3076
  179.5 31.1 %copy-start.6 = (s32[1,20,128]{2,0,1:T(1,128)S(1)}, s32[1,20,128]{2,0,1:T(1,128)}, u32[]{:S(2)}) copy-start(s32[1,20,128]{2,0,1:T(1,128)} %param.16) | copy-start | bytes 30724
  179.5 31.2 %copy-start.7 = (s32[1,1,2048]{2,1,0:T(1,128)S(1)}, s32[1,1,2048]{2,1,0:T(1,128)}, u32[]{:S(2)}) copy-start(s32[1,1,2048]{2,1,0:T(1,128)} %param.19) | copy-start | bytes 24580
  179.5 5.7 collective-permute-start.2
  185.3 5.6 collective-permute-start.3
  191.0 5.6 collective-permute-start.4
  196.7 5.6 collective-permute-start.5
  202.3 5.6 collective-permute-start.6
  208.6 637.8 %all-reduce.3.cloned.1.call-start = ((), (), s32[]{:S(2)}) async-start(), calls=%async_computation.4 | async-start | bytes 1572864 | tf_op jit(solution)/shard_map/psum | solution.py:164
  356.7 9.0 %copy-start.10 = (f32[256]{0:T(256)S(1)}, f32[256]{0:T(256)}, u32[]{:S(2)}) copy-start(f32[256]{0:T(256)} %param.24) | copy-start | bytes 3076
  365.5 10.5 %copy-start.4 = (bf16[256,256]{1,0:T(8,128)(2,1)S(1)}, bf16[256,256]{1,0:T(8,128)(2,1)}, u32[]{:S(2)}) copy-start(bf16[256,256]{1,0:T(8,128)(2,1)} %copy.39) | copy-start | bytes 393220
  375.9 0.9 copy-start.3
  376.5 2.7 copy-start.5
  376.8 2.6 copy-start.12
  376.8 3.4 copy-start.13
Sparse Core Ops, SparseCore 0:
  208.7 138.1 all-gather.1
  382.8 463.6 all-reduce.2
where the time goes:
time: 858 us; the launch traced here: 857 us
  waiting for transfers between devices  742 us (86%)
  starting transfers between devices  42.2 us (5%)
  local copies, waits for them, and re-layouts  26.3 us (3%)
  other arithmetic  22.7 us (3%)
  between operations  14.6 us (2%)
  matrix products  9.08 us (1%)
    psum x1, waiting for transfers between devices, per_device(): grad_out, grad_pair = lax.psum((grad_out, grad_pair), ('tm', 'dp'))  463 us
    all_gather x1, waiting for transfers between devices, per_device(): full_table = lax.all_gather(memory_bf, 'dp', axis=0, tiled=True)  136 us
    all_to_all x1, waiting for transfers between devices, per_device(): lax.all_to_all(slot_sums.reshape(groups, per_owner, feat_width), 'dp', sp...  95.7 us
    ppermute x7, waiting for transfers between devices, shifted(): lax.ppermute(value, axis, [(source, source + steps) for source in range(i...  25.6 us
    all_to_all x1, starting transfers between devices, per_device(): lax.all_to_all(requests, 'dp', split_axis=0, concat_axis=0, tiled=True)  18.7 us
  transfers between devices with their start and end apart: 12, of which 12 were waited for; matrix products, arithmetic and copies ran while one was open for 1% of the time, Pallas kernels for 0%

commit v1 on v0

--- a/solution.py
+++ b/solution.py
@@ -90,6 +90,12 @@
     pred_weights,
     pred_out,
 ):
+
+    def deliver_shifts_all_up(inputs, bus_axis, shard_axis):
+        for c in (bus_axis, shard_axis):
+            inputs = lax.psum(inputs, c)
+        return inputs
+
     groups = lax.axis_size("dp")
     node_dev, feat_width = memory0.shape
     list_len = node_list.shape[2]
@@ -161,7 +167,7 @@
         pred_weights,
         pred_out,
     )
-    grad_out, grad_pair = lax.psum((grad_out, grad_pair), ("tm", "dp"))
+    grad_out, grad_pair = deliver_shifts_all_up((grad_out, grad_pair), "dp", "tm")
     return (logit_out[None, :], new_memory[None], grad_out, grad_pair)
 
 

time: 858 us -> 732 us (0.85)
  the two profiles are of different devices: /device:TPU:2 before, /device:TPU:8 now
where the time goes in v1:
time: 732 us; the launch traced here: 731 us
  waiting for transfers between devices  599 us (82%)
  starting transfers between devices  60 us (8%)
  local copies, waits for them, and re-layouts  26.3 us (4%)
  other arithmetic  22.7 us (3%)
  between operations  14.3 us (2%)
  matrix products  9.07 us (1%)
    psum x2, waiting for transfers between devices, deliver_shifts_all_up(): inputs = lax.psum(inputs, c)  339 us
    all_gather x1, waiting for transfers between devices, per_device(): full_table = lax.all_gather(memory_bf, 'dp', axis=0, tiled=True)  138 us
    all_to_all x1, waiting for transfers between devices, per_device(): lax.all_to_all(slot_sums.reshape(groups, per_owner, feat_width), 'dp', sp...  95.6 us
    ppermute x7, starting transfers between devices, shifted(): lax.ppermute(value, axis, [(source, source + steps) for source in range(i...  29.6 us
    all_to_all x1, starting transfers between devices, per_device(): lax.all_to_all(requests, 'dp', split_axis=0, concat_axis=0, tiled=True)  18.7 us
  transfers between devices with their start and end apart: 13, of which 13 were waited for; matrix products, arithmetic and copies ran while one was open for 2% of the time, Pallas kernels for 0%

profile of v1, /device:TPU:8, one launch (start us, length us, event | category | flops | bytes accessed | tf_op | source)
XLA Modules:
  0.0 731.2 jit_solution(3051501987258591559)
XLA Ops:
  7.7 1.4 broadcast_minimum_fusion
  9.1 0.7 all_to_all.15
  9.8 18.7 %all-to-all-start = ((s32[64,1,32]{2,1,0:T(1,128)}), s32[64,1,32]{2,1,0:T(1,128)S(1)}, u32[]{:S(2)}, u32[]{:S(2)}) async-start(s32[64,1,32]{2,1,0:T(1,128)} %bitcast.2), calls=%async_computation | async-start | bytes 65536 | tf_op jit(solution)/shard_map/all_to_all | solution.py:104
  28.5 0.7 compare_select_fusion.4
  29.2 1.9 scatter_custom_fusion.1
  31.1 0.7 all_to_all.18
  31.8 10.4 %all-to-all-done = s32[64,1,32]{2,1,0:T(1,128)S(1)} async-done(((s32[64,1,32]{2,1,0:T(1,128)}), s32[64,1,32]{2,1,0:T(1,128)S(1)}, u32[]{:S(2)}, u32[]{:S(2)}) %all-to-all-start) | async-done | bytes 8224 | tf_op jit(solution)/shard_map/all_to_all | solution.py:104
  42.2 5.3 all-to-all-start.2
  47.5 1.1 convolution_convert_fusion.1
  48.6 3.4 scatter_custom_fusion
  52.0 9.1 %all-to-all-done.2 = f32[64,1,32]{2,1,0:T(1,128)S(1)} async-done(((f32[64,1,32]{2,1,0:T(1,128)}), f32[64,1,32]{2,1,0:T(1,128)S(1)}, u32[]{:S(2)}, u32[]{:S(2)}) %all-to-all-start.2) | async-done | bytes 8224 | tf_op jit(solution)/shard_map/all_to_all | solution.py:125
  61.1 6.1 all-to-all-start.1
  67.3 0.7 reduce.12
  68.6 0.7 reduce.13
  70.0 95.6 %all-to-all-done.1 = f32[64,32,256]{2,1,0:T(8,128)S(1)} async-done(((f32[64,32,256]{2,1,0:T(8,128)}), f32[64,32,256]{2,1,0:T(8,128)S(1)}, u32[]{:S(2)}, u32[]{:S(2)}) %all-to-all-start.1) | async-done | bytes 2097184 | tf_op jit(solution)/shard_map/all_to_all | solution.py:118
  165.9 0.8 fusion.7
  166.7 1.0 convolution_add_fusion.1
  167.8 1.4 collective-permute-start
  169.3 0.9 collective-permute-done
  170.2 4.6 collective-permute-start.1
  174.8 0.9 collective-permute-done.1
  175.8 4.8 collective-permute-start.2
  180.7 0.9 collective-permute-done.2
  181.6 4.7 collective-permute-start.3
  186.3 0.9 collective-permute-done.3
  187.3 4.7 collective-permute-start.4
  192.0 0.9 collective-permute-done.4
  193.0 4.7 collective-permute-start.5
  197.7 0.9 collective-permute-done.5
  198.7 4.7 collective-permute-start.6
  203.4 0.9 collective-permute-done.6
  205.4 0.8 copy.39
  206.1 0.8 copy.40
  207.1 138.5 %all-gather.2.cloned.1.call-done = bf16[8192,256]{1,0:T(8,128)(2,1)} async-done(((bf16[128,256]{1,0:T(8,128)(2,1)}), bf16[8192,256]{1,0:T(8,128)(2,1)}) %all-gather.2.cloned.1.call-update) | async-done | bytes 4194320 | tf_op jit(solution)/shard_map/all_gather | solution.py:155
  345.5 9.4 %gather_fusion = bf16[2048,256]{1,0:T(8,128)(2,1)S(1)} fusion(bf16[8192,256]{1,0:T(8,128)(2,1)} %all-gather.2.cloned.1.call-done, s32[2048]{0:T(1024)S(1)} %broadcast_clamp_fusion), kind=kCustom, calls=%fused_computation | custom fusion | bytes 2105344 | tf_op jit(solution)/shard_map/jit(_take)/gather | solution.py:158
  355.4 7.6 %gather_fusion.2 = bf16[2560,256]{1,0:T(8,128)(2,1)S(1)} fusion(bf16[2048,256]{1,0:T(8,128)(2,1)S(1)} %broadcast_select_fusion, s32[3072]{0:T(1024)S(1)} %pad_clamp_fusion), kind=kCustom, calls=%fused_computation.2 | custom fusion | bytes 2631680 | tf_op jit(solution)/shard_map/jit(_take)/gather | solution.py:32
  362.9 1.2 gather_fusion.1
  364.4 10.1 %add_convert_fusion = bf16[20,128,256]{2,1,0:T(8,128)(2,1)S(1)} fusion(f32[256]{0:T(256)S(1)} %copy-done.10, f32[20,128]{1,0:T(8,128)S(1)} %bitcast.137, bf16[20,128,256]{2,1,0:T(8,128)(2,1)S(1)} %bitcast.127, pred[20,128]{1,0:T(8,128)(4,1)S(1)} %compare_and_fusion), kind=kLoop, calls=%fused_computation.7 | loop fusion | flops 3276800 | bytes 2635264 | tf_op jit(solution)/shard_map/convert_element_type | solution.py:34
  375.4 1.1 multiply_reduce_fusion
  376.7 1.1 fusion.1
  378.0 0.8 multiply_reduce_fusion.2
  379.3 1.1 convolution_bitcast_fusion.2
  380.4 0.8 pad_maximum_fusion
  381.3 263.8 %all-reduce.5.cloned.1.call-done = (f32[256,256]{1,0:T(8,128)}, f32[2,256,256]{2,1,0:T(8,128)}) async-done(((f32[256,256]{1,0:T(8,128)}, f32[2,256,256]{2,1,0:T(8,128)}), (f32[256,256]{1,0:T(8,128)}, f32[2,256,256]{2,1,0:T(8,128)})) %all-reduce.5.cloned.1.call-update) | async-done | bytes 786448 | tf_op jit(solution)/shard_map/psum | solution.py:96
  645.1 0.7 add_bitcast_fusion
  645.9 75.2 %all-reduce.7.cloned.1.call-done = (f32[256,256]{1,0:T(8,128)}, f32[2,256,256]{2,1,0:T(8,128)}) async-done(((f32[256,256]{1,0:T(8,128)}, f32[2,256,256]{2,1,0:T(8,128)}), (f32[256,256]{1,0:T(8,128)}, f32[2,256,256]{2,1,0:T(8,128)})) %all-reduce.7.cloned.1.call-update) | async-done | bytes 786448 | tf_op jit(solution)/shard_map/psum | solution.py:96
  721.1 1.7 copy.60
  722.8 1.9 copy.61
  (73 shorter events, 6.3 us)
Async XLA Ops:
  7.2 159.5 %copy-start = (bf16[256,512]{1,0:T(8,128)(2,1)S(1)}, bf16[256,512]{1,0:T(8,128)(2,1)}, u32[]{:S(2)}) copy-start(bf16[256,512]{1,0:T(8,128)(2,1)} %param.22) | copy-start | bytes 786436
  9.8 32.5 %all-to-all-start = ((s32[64,1,32]{2,1,0:T(1,128)}), s32[64,1,32]{2,1,0:T(1,128)S(1)}, u32[]{:S(2)}, u32[]{:S(2)}) async-start(s32[64,1,32]{2,1,0:T(1,128)} %bitcast.2), calls=%async_computation | async-start | bytes 65536 | tf_op jit(solution)/shard_map/all_to_all | solution.py:104
  42.2 18.9 %all-to-all-start.2 = ((f32[64,1,32]{2,1,0:T(1,128)}), f32[64,1,32]{2,1,0:T(1,128)S(1)}, u32[]{:S(2)}, u32[]{:S(2)}) async-start(f32[64,1,32]{2,1,0:T(1,128)} %bitcast.8), calls=%async_computation.2 | async-start | bytes 65536 | tf_op jit(solution)/shard_map/all_to_all | solution.py:125
  61.1 104.5 %all-to-all-start.1 = ((f32[64,32,256]{2,1,0:T(8,128)}), f32[64,32,256]{2,1,0:T(8,128)S(1)}, u32[]{:S(2)}, u32[]{:S(2)}) async-start(f32[64,32,256]{2,1,0:T(8,128)} %bitcast.6), calls=%async_computation.1 | async-start | bytes 4194304 | tf_op jit(solution)/shard_map/all_to_all | solution.py:118
  67.2 278.3 %all-gather.2.cloned.1.call-start = ((), (), s32[]{:S(2)}) async-start(), calls=%async_computation.3 | async-start | bytes 4259840 | tf_op jit(solution)/shard_map/all_gather | solution.py:155
  70.0 96.7 %copy-start.11 = (f32[512]{0:T(512)S(1)}, f32[512]{0:T(512)}, u32[]{:S(2)}) copy-start(f32[512]{0:T(512)} %param.23) | copy-start | bytes 6148
  165.9 1.8 copy-start.1
  167.7 37.5 %copy-start.8 = (s32[1,20,128]{2,0,1:T(1,128)S(1)}, s32[1,20,128]{2,0,1:T(1,128)}, u32[]{:S(2)}) copy-start(s32[1,20,128]{2,0,1:T(1,128)} %param.17) | copy-start | bytes 30724
  167.7 37.5 %copy-start.2 = (bf16[4,256,256]{2,1,0:T(8,128)(2,1)S(1)}, bf16[4,256,256]{2,1,0:T(8,128)(2,1)}, u32[]{:S(2)}) copy-start(bf16[4,256,256]{2,1,0:T(8,128)(2,1)} %param.25) | copy-start | bytes 1572868
  167.8 2.3 collective-permute-start
  170.2 5.4 collective-permute-start.1
  175.8 31.1 %copy-start.9 = (s32[1,2,128]{2,1,0:T(2,128)S(1)}, s32[1,2,128]{2,1,0:T(2,128)}, u32[]{:S(2)}) copy-start(s32[1,2,128]{2,1,0:T(2,128)} %param.15) | copy-start | bytes 3076
  175.8 31.1 %copy-start.6 = (s32[1,20,128]{2,0,1:T(1,128)S(1)}, s32[1,20,128]{2,0,1:T(1,128)}, u32[]{:S(2)}) copy-start(s32[1,20,128]{2,0,1:T(1,128)} %param.16) | copy-start | bytes 30724
  175.8 31.2 %copy-start.7 = (s32[1,1,2048]{2,1,0:T(1,128)S(1)}, s32[1,1,2048]{2,1,0:T(1,128)}, u32[]{:S(2)}) copy-start(s32[1,1,2048]{2,1,0:T(1,128)} %param.19) | copy-start | bytes 24580
  175.8 5.7 collective-permute-start.2
  181.6 5.6 collective-permute-start.3
  187.3 5.6 collective-permute-start.4
  193.0 5.6 collective-permute-start.5
  198.7 5.6 collective-permute-start.6
  204.9 440.2 %all-reduce.5.cloned.1.call-start = ((), (), s32[]{:S(2)}) async-start(), calls=%async_computation.4 | async-start | bytes 1572864 | tf_op jit(solution)/shard_map/psum | solution.py:96
  355.3 9.0 %copy-start.10 = (f32[256]{0:T(256)S(1)}, f32[256]{0:T(256)}, u32[]{:S(2)}) copy-start(f32[256]{0:T(256)} %param.24) | copy-start | bytes 3076
  364.1 10.5 %copy-start.4 = (bf16[256,256]{1,0:T(8,128)(2,1)S(1)}, bf16[256,256]{1,0:T(8,128)(2,1)}, u32[]{:S(2)}) copy-start(bf16[256,256]{1,0:T(8,128)(2,1)} %copy.39) | copy-start | bytes 393220
  374.5 0.9 copy-start.3
  375.1 2.7 copy-start.5
  375.4 2.5 copy-start.12
  375.4 3.4 copy-start.13
  381.3 339.9 %all-reduce.7.cloned.1.call-start = ((), (), s32[]{:S(2)}) async-start(), calls=%async_computation.5 | async-start | bytes 1572864 | tf_op jit(solution)/shard_map/psum | solution.py:96
Sparse Core Ops, SparseCore 0:
  205.1 140.4 all-gather.1
  381.4 263.6 all-reduce.4
  647.8 73.3 all-reduce.6
